TPU v7x, 128 devices: a whole 4x4x4 slice. The times are simulated.
128 devices in a mesh: leaf: 2 (over core), front: 64 (over z, y, x).
Axes of the slice: x: 4, y: 4, z: 4, core: 2. Of those that a mesh axis runs over, the one named last changes fastest.
Arguments:
- front_block: float32 [8192, 8192], P('leaf', 'front'), as said below
- child_update: float32 [2, 6144, 8192], P('leaf', None, 'front'), as said below
- child_map: int32 [2, 48], P('leaf'), may hold values from 0 to 63, as said below
Outputs:
- factored: float32 [8192, 8192], P('leaf', 'front')
Inputs may be any that keep to these rules, and one draw needn't show every extreme that they name: `child_map`: each row is strictly increasing, holds 48 distinct blocks, and always names block 0 and block 63. `front_block`: Symmetric; the assembled front is positive definite. `child_update`: each child's update is symmetric and positive semidefinite in the child's order; columns of parent blocks that the child's map does not name are zero.
All inputs are finite; a program needn't handle non-finite values.
Results may differ from a plain program's by a relative error of at most 0.000088.
Values sent between devices are 32-bit elements; how exact they have to be, the bound alone decides.
A program may use at most 128 MiB of HBM per device.

v0:
```python
import jax
import jax.numpy as jnp
from jax import lax
from jax.sharding import PartitionSpec as P

BLK = 128
S = 512
HIGHEST = lax.Precision.HIGHEST


def gather_half(blocks, child_map, half, half_blocks):
    parent = half * half_blocks + jnp.arange(half_blocks, dtype=jnp.int32)
    hit = child_map[None, :] == parent[:, None]
    found = jnp.any(hit, axis=1)
    index = jnp.argmax(hit, axis=1)
    picked = jnp.take(blocks, index, axis=0)
    picked = jnp.where(found[:, None, None], picked, jnp.zeros_like(picked))
    return picked.reshape(half_blocks * BLK, blocks.shape[2])


def per_device(front_block, child_update, child_map):
    rows, cols = front_block.shape
    n_leaf = lax.axis_size("leaf")
    n_front = lax.axis_size("front")
    leaf = lax.axis_index("leaf")
    front = lax.axis_index("front")
    half_blocks = rows // BLK
    blocks = child_update[0].reshape(-1, BLK, cols)
    cmap = child_map[0]
    own = gather_half(blocks, cmap, leaf, half_blocks)
    send = gather_half(blocks, cmap, 1 - leaf, half_blocks)
    recv = lax.ppermute(send, "leaf", [(0, 1), (1, 0)])
    first = jnp.where(leaf == 0, own, recv)
    second = jnp.where(leaf == 0, recv, own)
    assembled = front_block + first + second
    top = assembled[:S]
    piv_cols = S // cols
    is_piv = front < piv_cols
    col_at = jnp.minimum(front, piv_cols - 1) * cols
    panel = lax.dynamic_update_slice_in_dim(
        jnp.zeros((S, S), jnp.float32), jnp.where(is_piv, top, jnp.zeros_like(top)), col_at, 1
    )
    pivot = lax.psum(panel, "front")
    factor = jnp.linalg.cholesky(pivot)
    own_solved = lax.linalg.triangular_solve(factor, top, left_side=True, lower=True).T
    from_leaf0 = lax.ppermute(own_solved, "leaf", [(0, 1)])
    col_solved = jnp.where(leaf == 0, own_solved, from_leaf0)
    piece = rows // n_front
    per_block = BLK // piece
    pieces = []
    for part in range(per_block):
        pairs = []
        for lf in range(n_leaf):
            for k in range(n_front // per_block):
                src = lf * n_front + lf * half_blocks + k
                dst = lf * n_front + per_block * k + part
                pairs.append((src, dst))
        pieces.append(
            lax.ppermute(col_solved[part * piece : (part + 1) * piece], ("leaf", "front"), pairs)
        )
    my_piece = pieces[0]
    for part in range(1, per_block):
        my_piece = jnp.where(front % per_block == part, pieces[part], my_piece)
    row_solved = lax.all_gather(my_piece, "front", tiled=True)
    schur = assembled - jnp.dot(row_solved, col_solved.T, precision=HIGHEST)
    row_global = leaf * rows + jnp.arange(rows, dtype=jnp.int32)
    col_global = front * cols + jnp.arange(cols, dtype=jnp.int32)
    col_start = jnp.minimum(front * cols, S - cols)
    left_rows = lax.dynamic_slice_in_dim(row_solved, col_start, cols, 1)
    left_top = jnp.pad(
        lax.dynamic_slice_in_dim(factor, col_start, cols, 1), ((0, rows - S), (0, 0))
    )
    left_part = jnp.where(row_global[:, None] < S, left_top, left_rows)
    right_top = jnp.pad(col_solved.T, ((0, rows - S), (0, 0)))
    right_part = jnp.where(row_global[:, None] < S, right_top, schur)
    return jnp.where(col_global[None, :] < S, left_part, right_part)


def solution(mesh):
    return jax.shard_map(
        per_device,
        mesh=mesh,
        in_specs=(P("leaf", "front"), P("leaf", None, "front"), P("leaf", None)),
        out_specs=P("leaf", "front"),
        check_vma=False,
    )
```

profile of v0, /device:TPU:1, one launch (start us, length us, event | category | flops | bytes accessed | tf_op | source)
XLA Modules:
  0.0 471.3 jit_solution(12014427817205239228)
XLA Ops:
  6.5 1.5 compare_reduce_fusion
  8.1 0.8 compare_reduce_fusion.3
  8.9 1.4 compare_reduce_fusion.2
  10.3 2.0 gather_fusion.1
  12.3 3.2 select_select_fusion
  15.5 2.9 copy.84
  18.4 1.4 collective-permute-start
  19.9 2.0 gather_fusion
  21.8 3.2 select_select_fusion.1
  25.1 2.9 copy.83
  28.0 2.9 copy.56
  30.8 3.3 select_add_fusion
  34.1 1.4 broadcast_in_dim.58
  35.8 0.7 fusion.3
  37.1 129.3 %all-reduce.5.cloned.1.call-done = f32[512,512]{0,1:T(8,128)} async-done(((f32[512,512]{0,1:T(8,128)}), f32[512,512]{0,1:T(8,128)}) %all-reduce.5.cloned.1.call-update) | async-done | bytes 1048592 | tf_op jit(solution)/shard_map/psum | solution.py:43
  166.4 2.6 copy.57
  169.0 1.8 fusion
  170.8 1.0 copy-done.3
  171.8 11.7 %cholesky.103 = f32[128,128]{1,0:T(8,128)S(1)} custom-call(f32[128,128]{1,0:T(8,128)S(1)} %cholesky.263), custom_call_target="Cholesky" | custom-call | tf_op jit(solution)/shard_map/jit(cholesky)/cholesky | solution.py:44
  183.5 0.7 copy.58
  184.3 9.8 %custom-call.30 = f32[1,128,128]{1,2,0:T(8,128)S(1)} custom-call(f32[1,128,128]{2,1,0:T(8,128)S(1)} %get-tuple-element.55), custom_call_target="InvertDiagBlocksLowerTriangular" | custom-call | tf_op jit(solution)/shard_map/jit(cholesky)/cholesky | solution.py:44
  194.1 1.2 fusion.7
  195.3 1.9 convolution_subtract_fusion.1
  197.4 1.5 cholesky.267
  198.9 13.2 %cholesky.215 = f32[128,128]{1,0:T(8,128)} custom-call(f32[128,128]{1,0:T(8,128)} %cholesky.267), custom_call_target="Cholesky" | custom-call | tf_op jit(solution)/shard_map/jit(cholesky)/cholesky | solution.py:44
  212.1 1.5 copy.60
  213.6 1.5 select_reduce_fusion.2
  215.1 11.4 %custom-call.31 = f32[1,128,128]{1,2,0:T(8,128)} custom-call(f32[1,128,128]{2,1,0:T(8,128)} %get-tuple-element.53), custom_call_target="InvertDiagBlocksLowerTriangular" | custom-call | tf_op jit(solution)/shard_map/jit(cholesky)/cholesky | solution.py:44
  226.5 1.0 cholesky.222
  227.5 0.8 constant_dynamic-update-slice_fusion.2
  228.4 1.2 convolution_dynamic-update-slice_fusion
  229.5 1.0 copy-done.2
  230.6 1.5 convolution_subtract_fusion.2
  232.1 11.7 %cholesky.236 = f32[128,128]{1,0:T(8,128)S(1)} custom-call(f32[128,128]{1,0:T(8,128)S(1)} %cholesky.272), custom_call_target="Cholesky" | custom-call | tf_op jit(solution)/shard_map/jit(cholesky)/cholesky | solution.py:44
  244.6 9.8 %custom-call.32 = f32[1,128,128]{1,2,0:T(8,128)S(1)} custom-call(f32[1,128,128]{2,1,0:T(8,128)S(1)} %get-tuple-element.51), custom_call_target="InvertDiagBlocksLowerTriangular" | custom-call | tf_op jit(solution)/shard_map/jit(cholesky)/cholesky | solution.py:44
  254.4 0.9 convolution_dynamic-update-slice_fusion.1
  255.3 1.5 convolution_subtract_fusion.3
  256.8 11.9 %cholesky.253 = f32[128,128]{1,0:T(8,128)S(1)} custom-call(f32[128,128]{1,0:T(8,128)S(1)} %convolution_subtract_fusion.3), custom_call_target="Cholesky" | custom-call | tf_op jit(solution)/shard_map/jit(cholesky)/cholesky | solution.py:44
  274.7 1.6 fusion.1
  276.3 14.5 %while.1 = (s32[]{:T(128)}, f32[512,512]{0,1:T(8,128)}, s32[4,2]{0,1:T(2,128)S(1)}, f32[4,128,128]{2,1,0:T(8,128)}, s32[]{:T(128)}) while((s32[]{:T(128)}, f32[512,512]{0,1:T(8,128)}, s32[4,2]{0,1:T(2,128)S(1)}, f32[4,128,128]{2,1,0:T(8,128)}, s32[]{:T(128)}) %tuple.35), condition=%wide.while_cond, body=%wide.while_body.sunk | while | flops 2 | bytes 393329 | solution.py:45
  277.0 2.2 dynamic-slice.7
  280.6 2.2 dynamic-slice.7
  284.3 2.2 dynamic-slice.7
  287.9 2.2 dynamic-slice.7
  290.8 40.1 %custom-call.33 = f32[4,128,128]{1,2,0:T(8,128)S(1)} custom-call(f32[4,128,128]{2,1,0:T(8,128)} %get-tuple-element.17), custom_call_target="InvertDiagBlocksLowerTriangular" | custom-call | tf_op jit(solution)/shard_map/triangular_solve | solution.py:45
  331.7 1.1 fusion.26
  332.9 1.1 fusion.23
  334.1 1.2 fusion.25
  335.3 1.3 fusion.14
  336.6 1.2 fusion.22
  337.8 2.0 fusion.4
  339.9 1.1 fusion.21
  341.1 1.3 collective-permute-start.1
  342.4 4.9 %collective-permute-done.1 = f32[128,512]{1,0:T(8,128)S(1)} collective-permute-done((f32[128,512]{1,0:T(8,128)S(1)}, f32[128,512]{1,0:T(8,128)S(1)}, u32[]{:S(2)}, u32[]{:S(2)}) %collective-permute-start.1) | collective-permute-done | bytes 262176 | tf_op jit(solution)/shard_map/ppermute | solution.py:46
  347.2 0.9 broadcast_select_fusion
  348.8 1.3 collective-permute-start.3
  350.1 1.3 collective-permute-start.2
  351.4 4.8 %collective-permute-done.3 = f32[64,512]{1,0:T(8,128)S(1)} collective-permute-done((f32[64,512]{1,0:T(8,128)}, f32[64,512]{1,0:T(8,128)S(1)}, u32[]{:S(2)}, u32[]{:S(2)}) %collective-permute-start.3) | collective-permute-done | bytes 131104 | tf_op jit(solution)/shard_map/ppermute | solution.py:59
  357.0 1.7 constant_dynamic-slice_fusion.2
  358.7 80.8 %all-gather.2.cloned.1.call-done = f32[4096,512]{1,0:T(8,128)} async-done(((f32[64,512]{1,0:T(8,128)}), f32[4096,512]{1,0:T(8,128)}) %all-gather.2.cloned.1.call-update) | async-done | bytes 8388624 | tf_op jit(solution)/shard_map/all_gather | solution.py:64
  439.5 4.2 constant_dynamic-slice_fusion.1
  443.7 2.9 copy.86
  446.6 14.8 %select_select_fusion.2 = f32[4096,128]{0,1:T(8,128)} fusion(f32[512,128]{0,1:T(8,128)S(1)} %bitcast.58, f32[4096,128]{0,1:T(8,128)} %copy.86, f32[512,128]{0,1:T(8,128)} %constant_dynamic-slice_fusion.2, pred[128]{0:T(512)(128)(4,1)S(1)} %add_compare_fusion.1, pred[4096]{0:T(1024)(128)(4,1)S(1)} %add_compare_fusion, f32[4096,128]{0,1:T(8,128)} %copy-done.1, ...), kind=kOutput, calls=%fused_computation.7 | convolution fusion | flops 3223322624 | bytes 15470720 | tf_op jit(solution)/shard_map/dot_general | solution.py:65
  461.4 2.9 copy.75
  (66 shorter events, 13.3 us)
Async XLA Ops:
  6.5 3.8 copy-start
  6.5 159.9 %all-reduce.5.cloned.1.call-start = ((), (), s32[]{:S(2)}) async-start(), calls=%async_computation | async-start | bytes 2097152 | tf_op jit(solution)/shard_map/psum | solution.py:43
  18.4 12.4 %collective-permute-start = (f32[4096,128]{0,1:T(8,128)}, f32[4096,128]{0,1:T(8,128)}, u32[]{:S(2)}, u32[]{:S(2)}) collective-permute-start(f32[4096,128]{0,1:T(8,128)} %copy.84), channel_id=1, source_target_pairs={{0,64},{64,0},{1,65},{65,1},{2,66},{66,2},{3,67},{67,3},{4,68},{68... | collective-permute-start | bytes 6291464 | tf_op jit(solution)/shard_map/ppermute | solution.py:32
  34.1 1.7 copy-start.1
  36.6 403.0 %all-gather.2.cloned.1.call-start = ((), (), s32[]{:S(2)}) async-start(), calls=%async_computation.1 | async-start | bytes 8519680 | tf_op jit(solution)/shard_map/all_gather | solution.py:64
  170.8 1.0 copy-start.3
  197.4 31.0 %copy-start.4 = (f32[384,128]{1,0:T(8,128)S(1)}, f32[384,128]{1,0:T(8,128)}, u32[]{:S(2)}) copy-start(f32[384,128]{1,0:T(8,128)} %convolution_subtract_fusion.1) | copy-start | bytes 589828
  229.5 1.0 copy-start.2
  331.0 0.7 copy-start.6
  339.9 2.5 copy-start.5
  341.1 6.2 %collective-permute-start.1 = (f32[128,512]{1,0:T(8,128)S(1)}, f32[128,512]{1,0:T(8,128)S(1)}, u32[]{:S(2)}, u32[]{:S(2)}) collective-permute-start(f32[128,512]{1,0:T(8,128)S(1)} %maximum_bitcast_fusion), channel_id=1, source_target_pairs={{0,64},{1,65},{2,66},{3,67},{4,68},{5,69},{6,70},{7,71},{8,72},{9,... | collective-permute-start | bytes 786440 | tf_op jit(solution)/shard_map/ppermute | solution.py:46
  348.8 7.4 %collective-permute-start.3 = (f32[64,512]{1,0:T(8,128)}, f32[64,512]{1,0:T(8,128)S(1)}, u32[]{:S(2)}, u32[]{:S(2)}) collective-permute-start(f32[64,512]{1,0:T(8,128)} %get-tuple-element.48), channel_id=1, source_target_pairs={{0,0},{1,2},{2,4},{3,6},{4,8},{5,10},{6,12},{7,14},{8,16},{9,18},{... | collective-permute-start | bytes 393224 | tf_op jit(solution)/shard_map/ppermute | solution.py:59
  350.1 6.1 %collective-permute-start.2 = (f32[64,512]{1,0:T(8,128)}, f32[64,512]{1,0:T(8,128)}, u32[]{:S(2)}, u32[]{:S(2)}) collective-permute-start(f32[64,512]{1,0:T(8,128)} %get-tuple-element.49), channel_id=1, source_target_pairs={{0,1},{1,3},{2,5},{3,7},{4,9},{5,11},{6,13},{7,15},{8,17},{9,19},{... | collective-permute-start | bytes 393224 | tf_op jit(solution)/shard_map/ppermute | solution.py:59
Sparse Core Ops, SparseCore 0:
  36.7 129.7 all-reduce.4
  357.1 82.4 all-gather.1
where the time goes:
time: 476 us; the launch traced here: 471 us
  waiting for transfers between devices  220 us (46%)
  other arithmetic  143 us (30%)
  local copies, waits for them, and re-layouts  54 us (11%)
  matrix products  32.1 us (7%)
  between operations  16.5 us (3%)
  starting transfers between devices  5.81 us (1%)
    psum x1, waiting for transfers between devices, per_device(): pivot = lax.psum(panel, 'front')  129 us
    another operation x15, other arithmetic, per_device(): factor = jnp.linalg.cholesky(pivot)  83.8 us
    all_gather x1, waiting for transfers between devices, per_device(): row_solved = lax.all_gather(my_piece, 'front', tiled=True)  80.8 us
    another operation x3, other arithmetic, per_device(): lax.linalg.triangular_solve(factor, top, left_side=True, lower=True)  41.7 us
    dot_general x1, matrix products, per_device(): schur = assembled - jnp.dot(row_solved, col_solved.T, precision=HIGHEST)  14.8 us
    another operation x20, local copies, waits for them, and re-layouts  14.5 us
  transfers between devices with their start and end apart: 6, of which 4 were waited for; matrix products, arithmetic and copies ran while one was open for 3% of the time, Pallas kernels for 0%

commit v1 on v0

--- a/solution.py
+++ b/solution.py
@@ -6,6 +6,12 @@
 BLK = 128
 S = 512
 HIGHEST = lax.Precision.HIGHEST
+
+
+def summed_here(x, mesh_axis):
+    pieces = lax.all_gather(x, mesh_axis, axis=0, tiled=False)
+    result = pieces.sum(axis=0)
+    return result
 
 
 def gather_half(blocks, child_map, half, half_blocks):
@@ -40,7 +46,7 @@
     panel = lax.dynamic_update_slice_in_dim(
         jnp.zeros((S, S), jnp.float32), jnp.where(is_piv, top, jnp.zeros_like(top)), col_at, 1
     )
-    pivot = lax.psum(panel, "front")
+    pivot = summed_here(panel, "front")
     factor = jnp.linalg.cholesky(pivot)
     own_solved = lax.linalg.triangular_solve(factor, top, left_side=True, lower=True).T
     from_leaf0 = lax.ppermute(own_solved, "leaf", [(0, 1)])

time: 476 us -> 608 us (1.28)
  waiting for transfers between devices: 220 us -> 369 us
  local copies, waits for them, and re-layouts: 54 us -> 29 us
  other arithmetic: 143 us -> 160 us
    all_gather x0 -> x1, waiting for transfers between devices: none -> 279 us  [summed_here(): pieces = lax.all_gather(x, mesh_axis, axis=0, tiled=False)]
    psum x1 -> x0, waiting for transfers between devices: 129 us -> none  [per_device(): pivot = lax.psum(panel, 'front')]
    reduce_sum x0 -> x1, other arithmetic: none -> 22 us  [summed_here(): result = pieces.sum(axis=0)]
    unnamed x16 -> x8, local copies, waits for them, and re-layouts: 8.79 us -> 1.51 us
    another operation x20 -> x12, local copies, waits for them, and re-layouts: 14.5 us -> 14.1 us
  transfers between devices with their start and end apart: 6 -> 6, of which waited for: 4 -> 5; matrix products, arithmetic and copies ran while one was open for 3% -> 1% of each run, Pallas kernels for 0% -> 0%
where the time goes in v1:
time: 608 us; the launch traced here: 607 us
  waiting for transfers between devices  369 us (61%)
  other arithmetic  160 us (26%)
  local copies, waits for them, and re-layouts  29 us (5%)
  matrix products  26.9 us (4%)
  between operations  16.2 us (3%)
    all_gather x1, waiting for transfers between devices, summed_here(): pieces = lax.all_gather(x, mesh_axis, axis=0, tiled=False)  279 us
    another operation x15, other arithmetic, per_device(): factor = jnp.linalg.cholesky(pivot)  81.1 us
    all_gather x1, waiting for transfers between devices, per_device(): row_solved = lax.all_gather(my_piece, 'front', tiled=True)  77.4 us
    another operation x3, other arithmetic, per_device(): lax.linalg.triangular_solve(factor, top, left_side=True, lower=True)  42 us
    reduce_sum x1, other arithmetic, summed_here(): result = pieces.sum(axis=0)  22 us
    another operation x12, local copies, waits for them, and re-layouts  14.1 us
  transfers between devices with their start and end apart: 6, of which 5 were waited for; matrix products, arithmetic and copies ran while one was open for 1% of the time, Pallas kernels for 0%

profile of v1, /device:TPU:1, one launch (start us, length us, event | category | flops | bytes accessed | tf_op | source)
XLA Modules:
  0.0 606.6 jit_solution(4179081448976312932)
XLA Ops:
  6.5 1.5 compare_reduce_fusion
  8.1 1.4 compare_reduce_fusion.2
  9.4 0.8 compare_reduce_fusion.3
  10.3 2.0 gather_fusion.1
  12.3 3.2 select_select_fusion
  15.5 1.4 collective-permute-start
  16.9 2.0 gather_fusion
  18.9 2.0 select_select_fusion.1
  21.1 1.9 fusion.1
  23.0 1.2 broadcast_in_dim.60
  24.7 0.8 fusion.6
  25.5 278.8 %all-gather.3.cloned.1.call-done = f32[64,512,512]{2,1,0:T(8,128)} async-done(((f32[1,512,512]{2,1,0:T(8,128)}), f32[64,512,512]{2,1,0:T(8,128)}) %all-gather.3.cloned.1.call-update) | async-done | bytes 67108880 | tf_op jit(solution)/shard_map/all_gather | solution.py:12
  304.3 22.0 %reduce_sum.9 = f32[512,512]{1,0:T(8,128)} reduce(f32[64,512,512]{2,1,0:T(8,128)} %all-gather.3.cloned.1.call-done, f32[]{:T(128)} %constant.191.clone.1), dimensions={0}, to_apply=%region_4.6 | reduce | flops 16515072 | bytes 68157440 | tf_op jit(solution)/shard_map/reduce_sum | solution.py:13
  326.3 2.5 copy.8
  328.8 1.8 fusion.2
  330.6 1.0 copy-done.2
  331.6 11.7 %cholesky.103 = f32[128,128]{1,0:T(8,128)S(1)} custom-call(f32[128,128]{1,0:T(8,128)S(1)} %cholesky.263), custom_call_target="Cholesky" | custom-call | tf_op jit(solution)/shard_map/jit(cholesky)/cholesky | solution.py:50
  343.3 1.2 cholesky.222
  344.5 9.8 %custom-call.30 = f32[1,128,128]{1,2,0:T(8,128)S(1)} custom-call(f32[1,128,128]{2,1,0:T(8,128)S(1)} %get-tuple-element.43), custom_call_target="InvertDiagBlocksLowerTriangular" | custom-call | tf_op jit(solution)/shard_map/jit(cholesky)/cholesky | solution.py:50
  354.3 2.0 constant_dynamic-update-slice_fusion.1
  356.3 1.3 convolution_subtract_fusion.1
  357.5 11.7 %cholesky.215 = f32[128,128]{1,0:T(8,128)S(1)} custom-call(f32[128,128]{1,0:T(8,128)S(1)} %cholesky.267), custom_call_target="Cholesky" | custom-call | tf_op jit(solution)/shard_map/jit(cholesky)/cholesky | solution.py:50
  369.3 0.6 select_reduce_fusion.2
  369.9 0.7 compare_reduce_fusion.6
  370.6 0.6 compare_reduce_fusion.7
  371.2 10.0 %custom-call.31 = f32[1,128,128]{1,2,0:T(8,128)S(1)} custom-call(f32[1,128,128]{2,1,0:T(8,128)S(1)} %get-tuple-element.40), custom_call_target="InvertDiagBlocksLowerTriangular" | custom-call | tf_op jit(solution)/shard_map/jit(cholesky)/cholesky | solution.py:50
  381.2 0.9 convolution_dynamic-update-slice_fusion
  382.2 1.4 convolution_subtract_fusion.2
  383.6 11.7 %cholesky.236 = f32[128,128]{1,0:T(8,128)S(1)} custom-call(f32[128,128]{1,0:T(8,128)S(1)} %cholesky.272), custom_call_target="Cholesky" | custom-call | tf_op jit(solution)/shard_map/jit(cholesky)/cholesky | solution.py:50
  395.3 0.6 select_reduce_fusion.1
  396.0 0.6 compare_reduce_fusion.5
  396.6 9.8 %custom-call.32 = f32[1,128,128]{1,2,0:T(8,128)S(1)} custom-call(f32[1,128,128]{2,1,0:T(8,128)S(1)} %get-tuple-element.37), custom_call_target="InvertDiagBlocksLowerTriangular" | custom-call | tf_op jit(solution)/shard_map/jit(cholesky)/cholesky | solution.py:50
  406.4 0.8 convolution_dynamic-update-slice_fusion.1
  407.3 1.4 convolution_subtract_fusion.3
  408.7 11.7 %cholesky.253 = f32[128,128]{1,0:T(8,128)S(1)} custom-call(f32[128,128]{1,0:T(8,128)S(1)} %convolution_subtract_fusion.3), custom_call_target="Cholesky" | custom-call | tf_op jit(solution)/shard_map/jit(cholesky)/cholesky | solution.py:50
  420.4 0.7 select_reduce_fusion
  421.1 0.7 compare_reduce_fusion.4
  424.3 1.8 fusion.3
  426.1 14.1 %while.1 = (s32[]{:T(128)}, f32[512,512]{1,0:T(8,128)}, s32[4,2]{0,1:T(2,128)S(1)}, f32[4,128,128]{2,1,0:T(8,128)}, s32[]{:T(128)}) while((s32[]{:T(128)}, f32[512,512]{1,0:T(8,128)}, s32[4,2]{0,1:T(2,128)S(1)}, f32[4,128,128]{2,1,0:T(8,128)}, s32[]{:T(128)}) %tuple.34), condition=%wide.while_cond, body=%wide.while_body.sunk | while | flops 2 | bytes 132705 | solution.py:51
  426.2 0.6 fusion.45
  426.8 2.9 bitcast_dynamic-update-slice_fusion.2
  429.8 0.6 fusion.45
  430.4 2.9 bitcast_dynamic-update-slice_fusion.2
  433.9 2.9 bitcast_dynamic-update-slice_fusion.2
  437.4 2.8 bitcast_dynamic-update-slice_fusion.2
  440.2 40.1 %custom-call.33 = f32[4,128,128]{1,2,0:T(8,128)S(1)} custom-call(f32[4,128,128]{2,1,0:T(8,128)} %get-tuple-element.17), custom_call_target="InvertDiagBlocksLowerTriangular" | custom-call | tf_op jit(solution)/shard_map/triangular_solve | solution.py:51
  480.4 1.1 fusion.29
  481.5 1.0 fusion.26
  482.5 1.1 fusion.28
  483.7 1.2 fusion.17
  484.9 1.1 fusion.25
  486.0 1.2 fusion.7
  487.3 1.1 fusion.24
  488.4 1.3 collective-permute-start.1
  489.7 2.9 collective-permute-done.1
  492.7 0.9 fusion.39
  493.5 1.3 collective-permute-start.2
  494.9 1.3 collective-permute-start.3
  496.2 9.8 %collective-permute-done.3 = f32[64,512]{0,1:T(8,128)} collective-permute-done((f32[64,512]{0,1:T(8,128)}, f32[64,512]{0,1:T(8,128)}, u32[]{:S(2)}, u32[]{:S(2)}) %collective-permute-start.3) | collective-permute-done | bytes 131104 | tf_op jit(solution)/shard_map/ppermute | solution.py:65
  506.0 1.7 broadcast_select_fusion.1
  507.7 1.7 copy.9
  509.4 1.9 constant_dynamic-slice_fusion.1
  511.3 77.4 %all-gather.5.cloned.1.call-done = f32[4096,512]{1,0:T(8,128)} async-done(((f32[64,512]{1,0:T(8,128)}), f32[4096,512]{1,0:T(8,128)}) %all-gather.5.cloned.1.call-update) | async-done | bytes 8388624 | tf_op jit(solution)/shard_map/all_gather | solution.py:70
  588.7 11.1 %select_select_fusion.2 = f32[4096,128]{1,0:T(8,128)} fusion(f32[512,128]{1,0:T(8,128)S(1)} %bitcast.70, f32[4096,512]{1,0:T(8,128)} %all-gather.5.cloned.1.call-done, s32[]{:T(128)S(6)} %select_n.94, f32[512,128]{1,0:T(8,128)} %constant_dynamic-slice_fusion.1, pred[4096]{0:T(1024)(128)(4,1)S(1)} %add_compare_fusion, ...), kind=kOutput, calls=%fused_computation.11 | convolution fusion | flops 3223322624 | bytes 15470724 | tf_op jit(solution)/shard_map/dot_general | solution.py:71
  (37 shorter events, 2.4 us)
Async XLA Ops:
  6.5 3.8 copy-start
  6.5 297.7 %all-gather.3.cloned.1.call-start = ((), (), s32[]{:S(2)}) async-start(), calls=%async_computation | async-start | bytes 68157440 | tf_op jit(solution)/shard_map/all_gather | solution.py:12
  15.5 5.6 collective-permute-start
  18.9 2.2 copy-start.3
  23.0 1.7 copy-start.1
  25.4 563.3 %all-gather.5.cloned.1.call-start = ((), (), s32[]{:S(2)}) async-start(), calls=%async_computation.1 | async-start | bytes 8519680 | tf_op jit(solution)/shard_map/all_gather | solution.py:70
  330.6 1.0 copy-start.2
  488.4 4.2 collective-permute-start.1
  493.5 2.7 collective-permute-start.2
  494.9 11.1 %collective-permute-start.3 = (f32[64,512]{0,1:T(8,128)}, f32[64,512]{0,1:T(8,128)}, u32[]{:S(2)}, u32[]{:S(2)}) collective-permute-start(f32[64,512]{0,1:T(8,128)} %get-tuple-element.32), channel_id=1, source_target_pairs={{0,0},{1,2},{2,4},{3,6},{4,8},{5,10},{6,12},{7,14},{8,16},{9,18},{... | collective-permute-start | bytes 393224 | tf_op jit(solution)/shard_map/ppermute | solution.py:65
Sparse Core Ops, SparseCore 0:
  25.6 278.6 all-gather.2
  509.5 79.1 all-gather.4
